TPU v7x, 256 devices: a whole 4x4x8 slice. The times are simulated.
256 devices in a mesh: row: 32 (over x, z), col: 8 (over y, core).
Axes of the slice: x: 4, y: 4, z: 8, core: 2. Of those that a mesh axis runs over, the one named last changes fastest.
Arguments:
- tensor: bfloat16 [64, 2048, 2048], P(None, 'row', 'col'), may hold values from -6 to 6
- pattern: int32 [32, 32], P('col', 'row'), may hold values 0 or 1
- coef: bfloat16 [2048, 2048], P('row', 'col'), may hold values from -0.1875 to 0.1875
Outputs:
- contracted: bfloat16 [64, 2048, 2048], P(None, 'row', 'col')
All inputs are finite; a program needn't handle non-finite values. No bound on the sum of `pattern` on one device may be relied on, other than what follows from the above.
Results may differ from a plain program's by a relative error of at most 0.001.
Values may be sent and summed in bfloat16 or wider, within the bound.
A program may use at most 64 MiB of HBM per device.

v0:
```python
import jax
import jax.numpy as jnp
from jax import lax
from jax.sharding import PartitionSpec as P


def per_device(tensor, pattern, coef):
    mu_all, nu_loc, aux_loc = tensor.shape
    atoms_aux, atoms_nu = pattern.shape
    blk = aux_loc // atoms_aux
    keep = jnp.transpose(pattern).astype(jnp.bfloat16)[None, :, None, :, None]
    masked = (tensor.reshape(mu_all, atoms_nu, blk, atoms_aux, blk) * keep).reshape(
        mu_all, nu_loc, aux_loc
    )
    matrix = lax.all_to_all(masked, "row", split_axis=0, concat_axis=1, tiled=True)
    form = "mna,no->moa"
    panel = lax.all_gather(coef, "col", axis=1, tiled=True)
    whole = lax.all_gather(panel, "row", axis=0, tiled=True)
    product = jnp.einsum(form, matrix, whole, preferred_element_type=jnp.float32)
    result = product.astype(jnp.bfloat16)
    return lax.all_to_all(result, "row", split_axis=1, concat_axis=0, tiled=True)


def solution(mesh):
    return jax.shard_map(
        per_device,
        mesh=mesh,
        in_specs=(P(None, "row", "col"), P("col", "row"), P("row", "col")),
        out_specs=P(None, "row", "col"),
        check_vma=False,
    )
```

profile of v0, /device:TPU:8, one launch (start us, length us, event | category | flops | bytes accessed | tf_op | source)
XLA Modules:
  0.0 217.4 jit_solution(12455503580650013508)
XLA Ops:
  6.5 0.0 all-gather.2.cloned.1.call-start
  6.5 14.4 %all_gather.6 = bf16[64,2048]{1,0:T(8,128)(2,1)} all-gather(bf16[64,256]{1,0:T(8,128)(2,1)} %param.5), channel_id=1, replica_groups=mesh['row'=32,'col'=8] {'col'}, dimensions={1}, use_global_device_ids=true | all-gather | bytes 294912 | tf_op jit(solution)/shard_map/all_gather | solution.py:17
  21.0 0.0 all-gather.2.cloned.1.call-update
  21.0 0.7 convert_bitcast_fusion
  21.7 0.1 mul.15
  21.7 0.1 mul.16
  21.8 1.7 broadcast_multiply_fusion
  23.5 72.5 %all_to_all.36 = bf16[64,64,256]{2,1,0:T(8,128)(2,1)S(1)} all-to-all(bf16[64,64,256]{2,1,0:T(8,128)(2,1)S(1)} %broadcast_multiply_fusion), channel_id=1, replica_groups=mesh['row'=32,'col'=8] {'row'}, dimensions={0} | all-to-all | bytes 4194304 | tf_op jit(solution)/shard_map/all_to_all | solution.py:15
  96.1 0.1 copy.12
  96.2 41.9 %all-gather.2.cloned.1.call-done = bf16[2048,2048]{1,0:T(8,128)(2,1)} async-done(((bf16[64,2048]{1,0:T(8,128)(2,1)}), bf16[2048,2048]{1,0:T(8,128)(2,1)}) %all-gather.2.cloned.1.call-update) | async-done | bytes 8388624 | tf_op jit(solution)/shard_map/all_gather | solution.py:18
  138.1 9.1 %fusion.5 = bf16[2,2048,256]{1,2,0:T(8,128)(2,1)} fusion(bf16[2,2048,256]{2,1,0:T(8,128)(2,1)S(1)} %bitcast.22, bf16[2048,2048]{1,0:T(8,128)(2,1)} %all-gather.2.cloned.1.call-done), kind=kOutput, calls=%fused_computation.3 | convolution fusion | flops 4296015872 | bytes 12582912 | tf_op jit(solution)/shard_map/mna,no->moa/dot_general | solution.py:19
  147.2 4.8 %copy.14 = bf16[2,2048,256]{2,0,1:T(2,128)(2,1)S(1)} copy(bf16[2,2048,256]{1,2,0:T(8,128)(2,1)} %fusion.5) | data formatting | bytes 4194304 | tf_op jit(solution)/shard_map/convert_element_type | solution.py:20
  152.0 56.7 %all_to_all.37 = bf16[2,2048,256]{2,0,1:T(2,128)(2,1)S(1)} all-to-all(bf16[2,2048,256]{2,0,1:T(2,128)(2,1)S(1)} %copy.14), channel_id=1, replica_groups=mesh['row'=32,'col'=8] {'row'}, dimensions={1} | all-to-all | bytes 4194304 | tf_op jit(solution)/shard_map/all_to_all | solution.py:21
  208.8 0.3 copy.15
  209.1 1.5 copy.16
Async XLA Ops:
  6.5 131.6 %all-gather.2.cloned.1.call-start = ((), (), s32[]{:S(2)}) async-start(), calls=%async_computation.2 | async-start | bytes 8650752 | tf_op jit(solution)/shard_map/all_gather | solution.py:18
Sparse Core Ops, SparseCore 0:
  21.1 116.9 all-gather.1
where the time goes:
time: 218 us; the launch traced here: 217 us
  blocking collectives  144 us (66%)
  waiting for transfers between devices  41.9 us (19%)
  between operations  13.4 us (6%)
  matrix products  9.1 us (4%)
  local copies, waits for them, and re-layouts  6.85 us (3%)
  other arithmetic  2.39 us (1%)
    all_to_all x1, blocking collectives, per_device(): lax.all_to_all(masked, 'row', split_axis=0, concat_axis=1, tiled=True)  72.5 us
    all_to_all x1, blocking collectives, per_device(): lax.all_to_all(result, 'row', split_axis=1, concat_axis=0, tiled=True)  56.7 us
    all_gather x1, waiting for transfers between devices, per_device(): whole = lax.all_gather(panel, 'row', axis=0, tiled=True)  41.9 us
    all_gather x1, blocking collectives, per_device(): panel = lax.all_gather(coef, 'col', axis=1, tiled=True)  14.4 us
    dot_general x1, matrix products, per_device(): jnp.einsum(form, matrix, whole, preferred_element_type=jnp.float32)  9.1 us
    convert_element_type x1, local copies, waits for them, and re-layouts, per_device(): result = product.astype(jnp.bfloat16)  4.82 us
  transfers between devices with their start and end apart: 1, of which 1 were waited for; matrix products, arithmetic and copies ran while one was open for 1% of the time, Pallas kernels for 0%

commit v1 on v0

--- a/solution.py
+++ b/solution.py
@@ -14,7 +14,26 @@
     )
     matrix = lax.all_to_all(masked, "row", split_axis=0, concat_axis=1, tiled=True)
     form = "mna,no->moa"
-    panel = lax.all_gather(coef, "col", axis=1, tiled=True)
+    piece_now, after, piece_next = (lax.axis_size("col"), lax.axis_index("col"), coef.shape[1])
+    parts_seen = [p * piece_now if m == 1 else p for m, p in enumerate(coef.shape)]
+    carry_out = main = coef
+    to_i = 1
+    panel = lax.dynamic_update_slice_in_dim(
+        jnp.zeros(parts_seen, coef.dtype), coef, after * piece_next, axis=1
+    )
+    while to_i < piece_now // 2 + 1:
+        carry_out = lax.ppermute(
+            carry_out, "col", [(m, (m + 1) % piece_now) for m in range(piece_now)]
+        )
+        panel = lax.dynamic_update_slice_in_dim(
+            panel, carry_out, (after - to_i) % piece_now * piece_next, axis=1
+        )
+        if 2 * to_i < piece_now:
+            main = lax.ppermute(main, "col", [(m, (m - 1) % piece_now) for m in range(piece_now)])
+            panel = lax.dynamic_update_slice_in_dim(
+                panel, main, (after + to_i) % piece_now * piece_next, axis=1
+            )
+        to_i += 1
     whole = lax.all_gather(panel, "row", axis=0, tiled=True)
     product = jnp.einsum(form, matrix, whole, preferred_element_type=jnp.float32)
     result = product.astype(jnp.bfloat16)

time: 218 us -> 228 us (1.046)
  blocking collectives: 144 us -> 128 us
  waiting for transfers between devices: 41.9 us -> 53.9 us
  local copies, waits for them, and re-layouts: 6.85 us -> 16.4 us
  starting transfers between devices: 0.01 us -> 5.14 us
    all_gather x1 -> x0, blocking collectives: 14.4 us -> none  [per_device(): panel = lax.all_gather(coef, 'col', axis=1, tiled=True)]
    convert_element_type x1, local copies, waits for them, and re-layouts: 4.82 us -> 12.8 us  [per_device(): result = product.astype(jnp.bfloat16)]
    ppermute x0 -> x7, waiting for transfers between devices: none -> 7.92 us  [the longest x4 7.8 us: per_device(): lax.ppermute(carry_out, 'col', [(m, (m + 1) % piece_now) for m in range(p...]
    ppermute x0 -> x7, starting transfers between devices: none -> 5.14 us  [the longest x3 5.12 us: per_device(): lax.ppermute(main, 'col', [(m, (m - 1) % piece_now) for m in range(piece_...]
    all_gather x1, waiting for transfers between devices: 41.9 us -> 46 us  [per_device(): whole = lax.all_gather(panel, 'row', axis=0, tiled=True)]
  transfers between devices with their start and end apart: 1 -> 8, of which waited for: 1 -> 6; matrix products, arithmetic and copies ran while one was open for 1% -> 2% of each run, Pallas kernels for 0% -> 0%
where the time goes in v1:
time: 228 us
  blocking collectives  128 us (56%)
  waiting for transfers between devices  53.9 us (24%)
  local copies, waits for them, and re-layouts  16.4 us (7%)
  between operations  13.5 us (6%)
  matrix products  8.48 us (4%)
  starting transfers between devices  5.14 us (2%)
  other arithmetic  2.39 us (1%)
    all_to_all x1, blocking collectives, per_device(): lax.all_to_all(masked, 'row', split_axis=0, concat_axis=1, tiled=True)  71.4 us
    all_to_all x1, blocking collectives, per_device(): lax.all_to_all(result, 'row', split_axis=1, concat_axis=0, tiled=True)  56.3 us
    all_gather x1, waiting for transfers between devices, per_device(): whole = lax.all_gather(panel, 'row', axis=0, tiled=True)  46 us
    convert_element_type x1, local copies, waits for them, and re-layouts, per_device(): result = product.astype(jnp.bfloat16)  12.8 us
    dot_general x1, matrix products, per_device(): jnp.einsum(form, matrix, whole, preferred_element_type=jnp.float32)  8.48 us
    ppermute x4, waiting for transfers between devices, per_device(): lax.ppermute(carry_out, 'col', [(m, (m + 1) % piece_now) for m in range(p...  7.8 us
    ppermute x3, starting transfers between devices, per_device(): lax.ppermute(main, 'col', [(m, (m - 1) % piece_now) for m in range(piece_...  5.12 us
  transfers between devices with their start and end apart: 8, of which 6 were waited for; matrix products, arithmetic and copies ran while one was open for 2% of the time, Pallas kernels for 0%

profile of v1, /device:TPU:8, one launch (start us, length us, event | category | flops | bytes accessed | tf_op | source)
XLA Modules:
  0.0 227.5 jit_solution(15837384356146931166)
XLA Ops:
  6.5 0.0 all-gather.2.cloned.1.call-start
  6.5 0.0 collective-permute-start
  6.5 1.7 collective-permute-start.1
  8.3 0.8 constant_dynamic-update-slice_fusion.7
  9.1 1.0 collective-permute-done
  10.1 0.0 collective-permute-start.2
  10.1 0.1 collective-permute-done.1
  10.2 1.6 collective-permute-start.3
  11.9 1.6 collective-permute-done.2
  13.4 0.0 collective-permute-start.4
  13.4 0.0 collective-permute-done.3
  13.4 1.7 collective-permute-start.5
  15.2 1.6 collective-permute-done.4
  16.8 0.0 collective-permute-start.6
  16.8 0.0 collective-permute-done.5
  16.8 3.6 %collective-permute-done.6 = bf16[64,256]{1,0:T(8,128)(2,1)S(1)} collective-permute-done((bf16[64,256]{1,0:T(8,128)(2,1)S(1)}, bf16[64,256]{1,0:T(8,128)(2,1)S(1)}, u32[]{:S(2)}, u32[]{:S(2)}) %collective-permute-start.6) | collective-permute-done | bytes 32800 | tf_op jit(solution)/shard_map/ppermute | solution.py:25
  20.5 0.0 copy-start
  20.5 0.7 copy-done
  21.2 0.0 all-gather.2.cloned.1.call-update
  21.2 0.7 convert_bitcast_fusion
  21.8 0.1 mul.47
  21.9 0.1 mul.48
  22.0 1.7 broadcast_multiply_fusion
  23.7 71.4 %all_to_all.36 = bf16[64,64,256]{2,1,0:T(8,128)(2,1)S(1)} all-to-all(bf16[64,64,256]{2,1,0:T(8,128)(2,1)S(1)} %broadcast_multiply_fusion), channel_id=1, replica_groups=mesh['row'=32,'col'=8] {'row'}, dimensions={0} | all-to-all | bytes 4194304 | tf_op jit(solution)/shard_map/all_to_all | solution.py:15
  95.2 0.1 copy.6
  95.3 46.0 %all-gather.2.cloned.1.call-done = bf16[2048,2048]{1,0:T(8,128)(2,1)} async-done(((bf16[64,2048]{1,0:T(8,128)(2,1)}), bf16[2048,2048]{1,0:T(8,128)(2,1)}) %all-gather.2.cloned.1.call-update) | async-done | bytes 8388624 | tf_op jit(solution)/shard_map/all_gather | solution.py:37
  141.3 8.5 %fusion.5 = bf16[2,2048,256]{2,1,0:T(8,128)(2,1)S(1)} fusion(bf16[2,2048,256]{2,1,0:T(8,128)(2,1)S(1)} %bitcast.22, bf16[2048,2048]{1,0:T(8,128)(2,1)} %all-gather.2.cloned.1.call-done), kind=kOutput, calls=%fused_computation.3 | convolution fusion | flops 4296015872 | bytes 12582912 | tf_op jit(solution)/shard_map/mna,no->moa/dot_general | solution.py:38
  149.8 12.8 %copy.7 = bf16[2,2048,256]{2,0,1:T(2,128)(2,1)S(1)} copy(bf16[2,2048,256]{2,1,0:T(8,128)(2,1)S(1)} %fusion.5) | data formatting | bytes 4194304 | tf_op jit(solution)/shard_map/convert_element_type | solution.py:39
  162.6 56.3 %all_to_all.37 = bf16[2,2048,256]{2,0,1:T(2,128)(2,1)S(1)} all-to-all(bf16[2,2048,256]{2,0,1:T(2,128)(2,1)S(1)} %copy.7), channel_id=1, replica_groups=mesh['row'=32,'col'=8] {'row'}, dimensions={1} | all-to-all | bytes 4194304 | tf_op jit(solution)/shard_map/all_to_all | solution.py:40
  218.9 1.8 copy.8
  (8 shorter events, 0.1 us)
Async XLA Ops:
  6.5 134.8 %all-gather.2.cloned.1.call-start = ((), (), s32[]{:S(2)}) async-start(), calls=%async_computation.2 | async-start | bytes 8650752 | tf_op jit(solution)/shard_map/all_gather | solution.py:37
  6.5 3.6 %collective-permute-start = (bf16[64,256]{1,0:T(8,128)(2,1)}, bf16[64,256]{1,0:T(8,128)(2,1)S(1)}, u32[]{:S(2)}, u32[]{:S(2)}) collective-permute-start(bf16[64,256]{1,0:T(8,128)(2,1)} %param.5), channel_id=1, source_target_pairs={{0,1},{1,2},{2,3},{3,4},{4,5},{5,6},{6,7},{7,0},{8,9},{9,10},{10,1... | collective-permute-start | bytes 98312 | tf_op jit(solution)/shard_map/ppermute | solution.py:25
  6.5 3.7 %collective-permute-start.1 = (bf16[64,256]{1,0:T(8,128)(2,1)}, bf16[64,256]{1,0:T(8,128)(2,1)S(1)}, u32[]{:S(2)}, u32[]{:S(2)}) collective-permute-start(bf16[64,256]{1,0:T(8,128)(2,1)} %param.5), channel_id=1, source_target_pairs={{0,7},{1,0},{2,1},{3,2},{4,3},{5,4},{6,5},{7,6},{8,15},{9,8},{10,9... | collective-permute-start | bytes 98312 | tf_op jit(solution)/shard_map/ppermute | solution.py:32
  10.1 3.3 %collective-permute-start.2 = (bf16[64,256]{1,0:T(8,128)(2,1)S(1)}, bf16[64,256]{1,0:T(8,128)(2,1)S(1)}, u32[]{:S(2)}, u32[]{:S(2)}) collective-permute-start(bf16[64,256]{1,0:T(8,128)(2,1)S(1)} %collective-permute-done), channel_id=1, source_target_pairs={{0,1},{1,2},{2,3},{3,4},{4,5},{5,6},{6,7},{7,0},{8,9},{9,10},{10,1... | collective-permute-start | bytes 98312 | tf_op jit(solution)/shard_map/ppermute | solution.py:25
  10.2 3.2 %collective-permute-start.3 = (bf16[64,256]{1,0:T(8,128)(2,1)S(1)}, bf16[64,256]{1,0:T(8,128)(2,1)S(1)}, u32[]{:S(2)}, u32[]{:S(2)}) collective-permute-start(bf16[64,256]{1,0:T(8,128)(2,1)S(1)} %collective-permute-done.1), channel_id=1, source_target_pairs={{0,7},{1,0},{2,1},{3,2},{4,3},{5,4},{6,5},{7,6},{8,15},{9,8},{10,9... | collective-permute-start | bytes 98312 | tf_op jit(solution)/shard_map/ppermute | solution.py:32
  13.4 3.3 %collective-permute-start.4 = (bf16[64,256]{1,0:T(8,128)(2,1)S(1)}, bf16[64,256]{1,0:T(8,128)(2,1)S(1)}, u32[]{:S(2)}, u32[]{:S(2)}) collective-permute-start(bf16[64,256]{1,0:T(8,128)(2,1)S(1)} %collective-permute-done.2), channel_id=1, source_target_pairs={{0,1},{1,2},{2,3},{3,4},{4,5},{5,6},{6,7},{7,0},{8,9},{9,10},{10,1... | collective-permute-start | bytes 98312 | tf_op jit(solution)/shard_map/ppermute | solution.py:25
  13.4 3.3 %collective-permute-start.5 = (bf16[64,256]{1,0:T(8,128)(2,1)S(1)}, bf16[64,256]{1,0:T(8,128)(2,1)S(1)}, u32[]{:S(2)}, u32[]{:S(2)}) collective-permute-start(bf16[64,256]{1,0:T(8,128)(2,1)S(1)} %collective-permute-done.3), channel_id=1, source_target_pairs={{0,7},{1,0},{2,1},{3,2},{4,3},{5,4},{6,5},{7,6},{8,15},{9,8},{10,9... | collective-permute-start | bytes 98312 | tf_op jit(solution)/shard_map/ppermute | solution.py:32
  16.8 3.7 %collective-permute-start.6 = (bf16[64,256]{1,0:T(8,128)(2,1)S(1)}, bf16[64,256]{1,0:T(8,128)(2,1)S(1)}, u32[]{:S(2)}, u32[]{:S(2)}) collective-permute-start(bf16[64,256]{1,0:T(8,128)(2,1)S(1)} %collective-permute-done.4), channel_id=1, source_target_pairs={{0,1},{1,2},{2,3},{3,4},{4,5},{5,6},{6,7},{7,0},{8,9},{9,10},{10,1... | collective-permute-start | bytes 98312 | tf_op jit(solution)/shard_map/ppermute | solution.py:25
  20.5 0.7 copy-start
Sparse Core Ops, SparseCore 0:
  21.3 119.9 all-gather.1
